TPU v7x, 32 devices: a whole 2x2x4 slice. The times are simulated.
32 devices in a mesh: batch: 4 (over y, x), proto: 8 (over z, core).
Axes of the slice: x: 2, y: 2, z: 4, core: 2. Of those that a mesh axis runs over, the one named last changes fastest.
Arguments:
- teacher_emb: bfloat16 [256, 2048], P('proto', 'batch'), may hold values from -22 to 22
- student_emb: bfloat16 [256, 2048], P('proto', 'batch'), may hold values from -6 to 6
- prototypes: bfloat16 [256, 65536], P('batch', 'proto'), may hold values from -16 to 16
Outputs:
- grad_proto: float32 [256, 65536], P('batch', 'proto')
- grad_student: float32 [256, 2048], P('proto', 'batch')
- loss: float32 [], replicated
All inputs are finite; a program needn't handle non-finite values.
Results may differ from a plain program's by a relative error of at most 0.00055.
The roundings to bfloat16 on the way count: a program that leaves them out, or rounds other values in their place, can miss the bound.
Values may be sent and summed in bfloat16 or wider, within the bound.
No kernel may reach another device: no remote copies, remote signals or barrier semaphores. Data moves between devices by JAX's collectives and lax.ppermute only.
A program may use at most 128 MiB of HBM per device.

v0:
```python
import jax
import jax.numpy as jnp
from jax import lax
from jax.sharding import PartitionSpec as P

ITERS = 3
teacher_temp = 0.07
student_temp = 0.1
epsilon = 1e-06


def unit(matrix):
    values = matrix.astype(jnp.float32)
    factor = lax.rsqrt(jnp.sum(values * values, axis=0, keepdims=True) + epsilon)
    return ((values * factor).astype(jnp.bfloat16), factor)


def cosine(left, right):
    return lax.dot_general(
        left, right, (((0,), (0,)), ((), ())), preferred_element_type=jnp.float32
    )


def shards(teacher_emb, student_emb, prototypes):
    teacher_full, student_full = (
        lax.all_gather(teacher_emb, "proto", axis=0, tiled=True),
        lax.all_gather(student_emb, "proto", axis=0, tiled=True),
    )
    proto_full = lax.all_gather(prototypes, "batch", axis=0, tiled=True)
    proto_unit, proto_scale = unit(proto_full)
    teacher_unit, unused = unit(teacher_full)
    student_unit, student_scale = unit(student_full)
    width = proto_full.shape[0]
    local_rows = teacher_full.shape[1]
    total_rows = local_rows * lax.axis_size("batch")
    expo = jnp.exp(cosine(teacher_unit, proto_unit) / teacher_temp)
    targets = expo
    for iteration in range(ITERS):
        column_total = lax.psum(jnp.sum(targets, axis=0), "batch")
        targets = targets / column_total[None, :]
        row_total = lax.psum(jnp.sum(targets, axis=1), "proto")
        targets = targets / row_total[:, None]
    cos_student = cosine(student_unit, proto_unit)
    logits = cos_student / student_temp
    partial_total = jnp.sum(jnp.exp(logits), axis=1)
    softmax_total = lax.psum(partial_total, "proto")
    logp = logits - jnp.log(softmax_total)[:, None]
    loss_part = -jnp.sum(targets * logp)
    loss = lax.psum(loss_part, ("batch", "proto")) / total_rows
    grad_logit = ((jnp.exp(logp) - targets) / (total_rows * student_temp)).astype(jnp.bfloat16)
    proto_rows = width // lax.axis_size("batch")
    crop_rows = width // lax.axis_size("proto")
    proto_start = lax.axis_index("batch") * proto_rows
    crop_start = lax.axis_index("proto") * crop_rows
    proto_own = lax.dynamic_slice_in_dim(proto_unit, proto_start, proto_rows, 0).astype(jnp.float32)
    student_own = lax.dynamic_slice_in_dim(student_unit, crop_start, crop_rows, 0).astype(
        jnp.float32
    )
    rows = student_unit
    proto_part = lax.psum_scatter(
        jnp.dot(rows, grad_logit, preferred_element_type=jnp.float32),
        "batch",
        scatter_dimension=0,
        tiled=True,
    )
    rows = proto_unit
    crop_part = lax.psum_scatter(
        lax.dot_general(
            rows, grad_logit, (((1,), (1,)), ((), ())), preferred_element_type=jnp.float32
        ),
        "proto",
        scatter_dimension=0,
        tiled=True,
    )
    proto_dot = lax.psum(jnp.sum(proto_own * proto_part, axis=0), "batch")
    crop_dot = lax.psum(jnp.sum(student_own * crop_part, axis=0), "proto")
    grad_proto = (proto_part - proto_own * proto_dot[None, :]) * proto_scale
    grad_student = (crop_part - student_own * crop_dot[None, :]) * student_scale
    return (grad_proto, grad_student, loss)


def solution(mesh):
    in_specs = (P("proto", "batch"), P("proto", "batch"), P("batch", "proto"))
    out_specs = (P("batch", "proto"), P("proto", "batch"), P())
    return jax.shard_map(shards, mesh=mesh, in_specs=in_specs, out_specs=out_specs, check_vma=False)
```

profile of v0, /device:TPU:0, one launch (start us, length us, event | category | flops | bytes accessed | tf_op | source)
XLA Modules:
  0.0 381.8 jit_solution(16406410473220215280)
XLA Ops:
  7.9 16.1 %all_gather.11 = bf16[256,512]{1,0:T(8,128)(2,1)S(1)} all-gather(bf16[32,512]{1,0:T(8,128)(2,1)} %param.3), channel_id=1, replica_groups=mesh['batch'=4,'proto'=8] {'proto'}, dimensions={0}, use_global_device_ids=true | all-gather | bytes 294912 | tf_op jit(solution)/shard_map/all_gather | solution.py:26
  24.1 14.4 %all_gather.9 = bf16[256,512]{1,0:T(8,128)(2,1)S(1)} all-gather(bf16[32,512]{1,0:T(8,128)(2,1)} %param.4), channel_id=1, replica_groups=mesh['batch'=4,'proto'=8] {'proto'}, dimensions={0}, use_global_device_ids=true | all-gather | bytes 294912 | tf_op jit(solution)/shard_map/all_gather | solution.py:27
  38.7 26.5 %all-gather.2.cloned.1.call-done = bf16[256,8192]{1,0:T(8,128)(2,1)} async-done(((bf16[64,8192]{1,0:T(8,128)(2,1)}), bf16[256,8192]{1,0:T(8,128)(2,1)}) %all-gather.2.cloned.1.call-update) | async-done | bytes 4194320 | tf_op jit(solution)/shard_map/all_gather | solution.py:29
  68.2 3.3 fusion.12
  73.6 7.2 %fusion.25 = (f32[8192]{0:T(1024)S(1)}, f32[512,8192]{1,0:T(8,128)}) fusion(bf16[256,8192]{1,0:T(8,128)(2,1)S(1)} %fusion.12, bf16[256,512]{1,0:T(8,128)(2,1)S(1)} %all_gather.11, f32[512]{0:T(512)S(1)} %add_rsqrt_fusion.1), kind=kOutput, calls=%fused_computation.44 | convolution fusion | flops 2156257280 | bytes 21268480 | tf_op jit(solution)/shard_map/dot_general | solution.py:19
  80.9 15.4 %psum.71 = f32[8192]{0:T(1024)S(1)} all-reduce(f32[8192]{0:T(1024)S(1)} %get-tuple-element.9), channel_id=1, replica_groups=mesh['batch'=4,'proto'=8] {'batch'}, use_global_device_ids=true, to_apply=%region_6.0 | all-reduce | flops 8192 | bytes 65536 | tf_op jit(solution)/shard_map/psum | solution.py:39
  96.3 7.0 %divide_reduce_fusion = f32[512]{0:T(512)S(1)} fusion(f32[512,8192]{1,0:T(8,128)} %get-tuple-element.10, f32[8192]{0:T(1024)S(1)} %psum.71), kind=kLoop, calls=%fused_computation.13 | loop fusion | flops 8388096 | bytes 16812032 | tf_op jit(solution)/shard_map/reduce_sum | solution.py:41
  103.3 13.6 %psum.72 = f32[512]{0:T(512)S(1)} all-reduce(f32[512]{0:T(512)S(1)} %divide_reduce_fusion), channel_id=1, replica_groups=mesh['batch'=4,'proto'=8] {'proto'}, use_global_device_ids=true, to_apply=%region_8.0 | all-reduce | flops 512 | bytes 4096 | tf_op jit(solution)/shard_map/psum | solution.py:41
  116.9 8.4 %fusion.7 = f32[8192]{0:T(1024)S(1)} fusion(f32[512,8192]{1,0:T(8,128)} %get-tuple-element.10, f32[512]{0:T(512)S(1)} %psum.72, f32[8192]{0:T(1024)S(1)} %psum.71), kind=kLoop, calls=%fused_computation.14 | loop fusion | flops 12574720 | bytes 16844800 | tf_op jit(solution)/shard_map/reduce_sum | solution.py:39
  125.3 15.1 %psum.73 = f32[8192]{0:T(1024)S(1)} all-reduce(f32[8192]{0:T(1024)S(1)} %fusion.7), channel_id=1, replica_groups=mesh['batch'=4,'proto'=8] {'batch'}, use_global_device_ids=true, to_apply=%region_10.0 | all-reduce | flops 8192 | bytes 65536 | tf_op jit(solution)/shard_map/psum | solution.py:39
  140.4 8.7 %fusion.8 = f32[512]{0:T(512)S(1)} fusion(f32[512,8192]{1,0:T(8,128)} %get-tuple-element.10, f32[8192]{0:T(1024)S(1)} %psum.73, f32[512]{0:T(512)S(1)} %psum.72, f32[8192]{0:T(1024)S(1)} %psum.71), kind=kLoop, calls=%fused_computation.15 | loop fusion | flops 16776704 | bytes 16846848 | tf_op jit(solution)/shard_map/reduce_sum | solution.py:41
  149.1 13.6 %psum.74 = f32[512]{0:T(512)S(1)} all-reduce(f32[512]{0:T(512)S(1)} %fusion.8), channel_id=1, replica_groups=mesh['batch'=4,'proto'=8] {'proto'}, use_global_device_ids=true, to_apply=%region_12.0 | all-reduce | flops 512 | bytes 4096 | tf_op jit(solution)/shard_map/psum | solution.py:41
  162.7 7.8 %fusion.9 = f32[8192]{0:T(1024)S(1)} fusion(f32[512,8192]{1,0:T(8,128)} %get-tuple-element.10, f32[512]{0:T(512)S(1)} %psum.74, f32[8192]{0:T(1024)S(1)} %psum.73, f32[512]{0:T(512)S(1)} %psum.72, f32[8192]{0:T(1024)S(1)} %psum.71), kind=kLoop, calls=%fused_computation.16 | loop fusion | flops 20963328 | bytes 16879616 | tf_op jit(solution)/shard_map/reduce_sum | solution.py:39
  170.5 15.3 %psum.75 = f32[8192]{0:T(1024)S(1)} all-reduce(f32[8192]{0:T(1024)S(1)} %fusion.9), channel_id=1, replica_groups=mesh['batch'=4,'proto'=8] {'batch'}, use_global_device_ids=true, to_apply=%region_14.0 | all-reduce | flops 8192 | bytes 65536 | tf_op jit(solution)/shard_map/psum | solution.py:39
  185.9 8.4 %fusion.10 = f32[512]{0:T(512)S(1)} fusion(f32[512,8192]{1,0:T(8,128)} %get-tuple-element.10, f32[8192]{0:T(1024)S(1)} %psum.75, f32[512]{0:T(512)S(1)} %psum.74, f32[8192]{0:T(1024)S(1)} %psum.73, f32[512]{0:T(512)S(1)} %psum.72, f32[8192]{0:T(1024)S(1)} %psum.71), kind=kLoop, calls=%fused_computation.17 | loop fusion | flops 25165312 | bytes 16881664 | tf_op jit(solution)/shard_map/reduce_sum | solution.py:41
  194.3 7.2 %exponential_reduce_fusion = (f32[512]{0:T(512)S(1)}, f32[512,8192]{1,0:T(8,128)}) fusion(bf16[256,512]{1,0:T(8,128)(2,1)S(1)} %fusion.17, bf16[256,8192]{1,0:T(8,128)(2,1)S(1)} %copy-done.1), kind=kOutput, calls=%fused_computation.12 | convolution fusion | flops 2155871744 | bytes 21235712 | tf_op jit(solution)/shard_map/dot_general | solution.py:19
  201.5 13.8 %all-reduce = (f32[512]{0:T(512)S(1)}, f32[512]{0:T(512)S(1)}) all-reduce(f32[512]{0:T(512)S(1)} %get-tuple-element.7, f32[512]{0:T(512)S(1)} %fusion.10), channel_id=1, replica_groups=mesh['batch'=4,'proto'=8] {'proto'}, use_global_device_ids=true, to_apply=%region_3.0 | all-reduce | flops 1024 | bytes 8192 | tf_op jit(solution)/shard_map/psum | solution.py:46
  215.3 15.3 %multiply_reduce_fusion = (f32[]{:T(128)}, bf16[512,8192]{1,0:T(8,128)(2,1)S(1)}) fusion(f32[512,8192]{1,0:T(8,128)} %get-tuple-element.8, f32[512]{0:T(512)S(1)} %log.3, f32[512,8192]{1,0:T(8,128)} %get-tuple-element.10, f32[512]{0:T(512)S(1)} %get-tuple-element.4, f32[8192]{0:T(1024)S(1)} %psum.75, f32[512]{0:T(512)S(1)} %psum.74, f32[8192]{0:T(1024)S(1)} %psum.73, ...), kind=kLoop, calls=%fused_computation.9 | loop fusion | flops 54525952 | bytes 42049540 | tf_op jit(solution)/shard_map/reduce_sum | solution.py:48
  237.0 9.0 %fusion.26 = f32[256,8192]{1,0:T(8,128)} fusion(bf16[256,512]{1,0:T(8,128)(2,1)S(1)} %fusion.17, bf16[512,8192]{1,0:T(8,128)(2,1)} %copy-done.3), kind=kOutput, calls=%fused_computation.45 | convolution fusion | flops 2147483648 | bytes 17039360 | tf_op jit(solution)/shard_map/dot_general | solution.py:61
  246.7 37.5 %psum.79 = f32[]{:T(128)} all-reduce(f32[]{:T(128)S(6)} %neg.3), channel_id=1, replica_groups=mesh['batch'=4,'proto'=8] {'batch','proto'}, use_global_device_ids=true, to_apply=%region_24.0 | all-reduce | flops 1 | bytes 8 | tf_op jit(solution)/shard_map/psum | solution.py:49
  285.8 15.5 %psum.78 = f32[512]{0:T(512)S(1)} all-reduce(f32[512]{0:T(512)S(1)} %fusion.22), channel_id=1, replica_groups=mesh['batch'=4,'proto'=8] {'proto'}, use_global_device_ids=true, to_apply=%region_22.0 | all-reduce | flops 512 | bytes 4096 | tf_op jit(solution)/shard_map/psum | solution.py:76
  302.7 50.4 %reduce-scatter.3.cloned.1.call-done = f32[64,8192]{1,0:T(8,128)} async-done(((f32[256,8192]{1,0:T(8,128)}), f32[64,8192]{1,0:T(8,128)}) %reduce-scatter.3.cloned.1.call-update) | async-done | bytes 2097168 | tf_op jit(solution)/shard_map/reduce_scatter | solution.py:60
  355.2 15.4 %psum.77 = f32[8192]{0:T(1024)S(1)} all-reduce(f32[8192]{0:T(1024)S(1)} %fusion.13), channel_id=1, replica_groups=mesh['batch'=4,'proto'=8] {'batch'}, use_global_device_ids=true, to_apply=%region_19.0 | all-reduce | flops 8192 | bytes 65536 | tf_op jit(solution)/shard_map/psum | solution.py:75
  370.6 3.5 fusion.15
  (27 shorter events, 17.1 us)
Async XLA Ops:
  7.2 58.0 %all-gather.2.cloned.1.call-start = ((), (), s32[]{:S(2)}) async-start(), calls=%async_computation.2 | async-start | bytes 5242880 | tf_op jit(solution)/shard_map/all_gather | solution.py:29
  7.9 277.0 %reduce-scatter.5.cloned.1.call-start = ((), (), s32[]{:S(2)}) async-start(), calls=%async_computation.4 | async-start | bytes 589824 | tf_op jit(solution)/shard_map/reduce_scatter | solution.py:67
  71.6 2.0 copy-start
  185.8 8.4 %copy-start.1 = (bf16[256,8192]{1,0:T(8,128)(2,1)S(1)}, bf16[256,8192]{1,0:T(8,128)(2,1)}, u32[]{:S(2)}) copy-start(bf16[256,8192]{1,0:T(8,128)(2,1)} %copy-done) | copy-start | bytes 12582916
  215.3 18.5 %copy-start.2 = (bf16[256,8192]{1,0:T(8,128)(2,1)S(1)}, bf16[256,8192]{1,0:T(8,128)(2,1)}, u32[]{:S(2)}) copy-start(bf16[256,8192]{1,0:T(8,128)(2,1)} %copy-done) | copy-start | bytes 12582916
  230.5 3.2 copy-start.3
  236.9 116.2 %reduce-scatter.3.cloned.1.call-start = ((), (), s32[]{:S(2)}) async-start(), calls=%async_computation.3 | async-start | bytes 10485760 | tf_op jit(solution)/shard_map/reduce_scatter | solution.py:60
Sparse Core Ops, SparseCore 0:
  9.8 55.2 all-gather.1
  237.0 27.9 reduce-scatter.4
  268.1 84.9 reduce-scatter.2
where the time goes:
time: 382 us
  blocking collectives  186 us (49%)
  waiting for transfers between devices  77.5 us (20%)
  other arithmetic  70.2 us (18%)
  matrix products  26.6 us (7%)
  between operations  16.3 us (4%)
  local copies, waits for them, and re-layouts  5.26 us (1%)
    reduce_scatter x1, waiting for transfers between devices, shards(): lax.psum_scatter(jnp.dot(rows, grad_logit, preferred_element_type=jnp.flo...  50.4 us
    psum x3, blocking collectives, shards(): column_total = lax.psum(jnp.sum(targets, axis=0), 'batch')  45.8 us
    psum x1, blocking collectives, shards(): loss = lax.psum(loss_part, ('batch', 'proto')) / total_rows  37.5 us
    psum x2, blocking collectives, shards(): row_total = lax.psum(jnp.sum(targets, axis=1), 'proto')  27.2 us
    all_gather x1, waiting for transfers between devices, shards(): proto_full = lax.all_gather(prototypes, 'batch', axis=0, tiled=True)  26.5 us
    reduce_sum x3, other arithmetic, shards(): row_total = lax.psum(jnp.sum(targets, axis=1), 'proto')  24.2 us
    reduce_sum x2, other arithmetic, shards(): column_total = lax.psum(jnp.sum(targets, axis=0), 'batch')  16.2 us
    all_gather x1, blocking collectives, shards(): lax.all_gather(teacher_emb, 'proto', axis=0, tiled=True)  16.1 us
  transfers between devices with their start and end apart: 3, of which 2 were waited for; matrix products, arithmetic and copies ran while one was open for 3% of the time, Pallas kernels for 0%

commit v1 on v0

--- a/solution.py
+++ b/solution.py
@@ -26,7 +26,14 @@
         lax.all_gather(teacher_emb, "proto", axis=0, tiled=True),
         lax.all_gather(student_emb, "proto", axis=0, tiled=True),
     )
-    proto_full = lax.all_gather(prototypes, "batch", axis=0, tiled=True)
+    ring = [prototypes]
+    for hop in range(3):
+        ring.append(lax.ppermute(ring[-1], "batch", [(dev, (dev + 1) % 4) for dev in range(4)]))
+    proto_full = jnp.roll(
+        jnp.concatenate(ring[::-1], axis=0),
+        (lax.axis_index("batch") + 1) * ring[0].shape[0],
+        axis=0,
+    )
     proto_unit, proto_scale = unit(proto_full)
     teacher_unit, unused = unit(teacher_full)
     student_unit, student_scale = unit(student_full)

time: 382 us -> 399 us (1.045)
  waiting for transfers between devices: 77.5 us -> 95 us
  other arithmetic: 70.2 us -> 65.6 us
    ppermute x0 -> x3, waiting for transfers between devices: none -> 43.7 us  [shards(): lax.ppermute(ring[-1], 'batch', [(dev, (dev + 1) % 4) for dev in range(4)])]
    all_gather x1 -> x0, waiting for transfers between devices: 26.5 us -> none  [shards(): proto_full = lax.all_gather(prototypes, 'batch', axis=0, tiled=True)]
  transfers between devices with their start and end apart: 3 -> 5, of which waited for: 2 -> 4; matrix products, arithmetic and copies ran while one was open for 3% -> 3% of each run, Pallas kernels for 0% -> 0%
where the time goes in v1:
time: 399 us; the launch traced here: 398 us
  blocking collectives  183 us (46%)
  waiting for transfers between devices  95 us (24%)
  other arithmetic  65.6 us (16%)
  matrix products  26.5 us (7%)
  between operations  16.7 us (4%)
  local copies, waits for them, and re-layouts  7.06 us (2%)
    reduce_scatter x1, waiting for transfers between devices, shards(): lax.psum_scatter(jnp.dot(rows, grad_logit, preferred_element_type=jnp.flo...  51.2 us
    psum x3, blocking collectives, shards(): column_total = lax.psum(jnp.sum(targets, axis=0), 'batch')  44.2 us
    ppermute x3, waiting for transfers between devices, shards(): lax.ppermute(ring[-1], 'batch', [(dev, (dev + 1) % 4) for dev in range(4)])  43.7 us
    psum x1, blocking collectives, shards(): loss = lax.psum(loss_part, ('batch', 'proto')) / total_rows  38 us
    psum x2, blocking collectives, shards(): row_total = lax.psum(jnp.sum(targets, axis=1), 'proto')  27.2 us
    reduce_sum x3, other arithmetic, shards(): row_total = lax.psum(jnp.sum(targets, axis=1), 'proto')  24.2 us
    reduce_sum x2, other arithmetic, shards(): column_total = lax.psum(jnp.sum(targets, axis=0), 'batch')  16.2 us
    psum x1, blocking collectives, shards(): crop_dot = lax.psum(jnp.sum(student_own * crop_part, axis=0), 'proto')  15.5 us
  transfers between devices with their start and end apart: 5, of which 4 were waited for; matrix products, arithmetic and copies ran while one was open for 3% of the time, Pallas kernels for 0%

profile of v1, /device:TPU:0, one launch (start us, length us, event | category | flops | bytes accessed | tf_op | source)
XLA Modules:
  0.0 398.0 jit_solution(7545715562320464752)
XLA Ops:
  10.2 24.3 %collective-permute-done = bf16[64,8192]{1,0:T(8,128)(2,1)S(1)} collective-permute-done((bf16[64,8192]{1,0:T(8,128)(2,1)}, bf16[64,8192]{1,0:T(8,128)(2,1)S(1)}, u32[]{:S(2)}, u32[]{:S(2)}) %collective-permute-start) | collective-permute-done | bytes 1048608 | tf_op jit(solution)/shard_map/ppermute | solution.py:31
  35.4 14.6 %all_gather.7 = bf16[256,512]{1,0:T(8,128)(2,1)S(1)} all-gather(bf16[32,512]{1,0:T(8,128)(2,1)} %param.3), channel_id=1, replica_groups=mesh['batch'=4,'proto'=8] {'proto'}, dimensions={0}, use_global_device_ids=true | all-gather | bytes 294912 | tf_op jit(solution)/shard_map/all_gather | solution.py:26
  50.0 9.8 %collective-permute-done.1 = bf16[64,8192]{1,0:T(8,128)(2,1)S(1)} collective-permute-done((bf16[64,8192]{1,0:T(8,128)(2,1)S(1)}, bf16[64,8192]{1,0:T(8,128)(2,1)S(1)}, u32[]{:S(2)}, u32[]{:S(2)}) %collective-permute-start.1) | collective-permute-done | bytes 1048608 | tf_op jit(solution)/shard_map/ppermute | solution.py:31
  59.8 14.5 %all_gather.6 = bf16[256,512]{1,0:T(8,128)(2,1)S(1)} all-gather(bf16[32,512]{1,0:T(8,128)(2,1)} %param.4), channel_id=1, replica_groups=mesh['batch'=4,'proto'=8] {'proto'}, dimensions={0}, use_global_device_ids=true | all-gather | bytes 294912 | tf_op jit(solution)/shard_map/all_gather | solution.py:27
  74.6 9.6 %collective-permute-done.2 = bf16[64,8192]{1,0:T(8,128)(2,1)S(1)} collective-permute-done((bf16[64,8192]{1,0:T(8,128)(2,1)S(1)}, bf16[64,8192]{1,0:T(8,128)(2,1)S(1)}, u32[]{:S(2)}, u32[]{:S(2)}) %collective-permute-start.2) | collective-permute-done | bytes 1048608 | tf_op jit(solution)/shard_map/ppermute | solution.py:31
  89.9 7.2 %fusion.25 = (f32[8192]{0:T(1024)S(1)}, f32[512,8192]{1,0:T(8,128)}) fusion(bf16[256,8192]{1,0:T(8,128)(2,1)S(1)} %fusion.12, bf16[256,512]{1,0:T(8,128)(2,1)S(1)} %all_gather.7, f32[512]{0:T(512)S(1)} %add_rsqrt_fusion.1), kind=kOutput, calls=%fused_computation.52 | convolution fusion | flops 2156257280 | bytes 21268480 | tf_op jit(solution)/shard_map/dot_general | solution.py:19
  97.1 14.0 %psum.71 = f32[8192]{0:T(1024)S(1)} all-reduce(f32[8192]{0:T(1024)S(1)} %get-tuple-element.9), channel_id=1, replica_groups=mesh['batch'=4,'proto'=8] {'batch'}, use_global_device_ids=true, to_apply=%region_6.7 | all-reduce | flops 8192 | bytes 65536 | tf_op jit(solution)/shard_map/psum | solution.py:46
  111.1 7.0 %divide_reduce_fusion = f32[512]{0:T(512)S(1)} fusion(f32[512,8192]{1,0:T(8,128)} %get-tuple-element.10, f32[8192]{0:T(1024)S(1)} %psum.71), kind=kLoop, calls=%fused_computation.13 | loop fusion | flops 8388096 | bytes 16812032 | tf_op jit(solution)/shard_map/reduce_sum | solution.py:48
  118.1 13.6 %psum.72 = f32[512]{0:T(512)S(1)} all-reduce(f32[512]{0:T(512)S(1)} %divide_reduce_fusion), channel_id=1, replica_groups=mesh['batch'=4,'proto'=8] {'proto'}, use_global_device_ids=true, to_apply=%region_8.9 | all-reduce | flops 512 | bytes 4096 | tf_op jit(solution)/shard_map/psum | solution.py:48
  131.7 8.4 %fusion.7 = f32[8192]{0:T(1024)S(1)} fusion(f32[512,8192]{1,0:T(8,128)} %get-tuple-element.10, f32[512]{0:T(512)S(1)} %psum.72, f32[8192]{0:T(1024)S(1)} %psum.71), kind=kLoop, calls=%fused_computation.14 | loop fusion | flops 12574720 | bytes 16844800 | tf_op jit(solution)/shard_map/reduce_sum | solution.py:46
  140.1 16.2 %psum.73 = f32[8192]{0:T(1024)S(1)} all-reduce(f32[8192]{0:T(1024)S(1)} %fusion.7), channel_id=1, replica_groups=mesh['batch'=4,'proto'=8] {'batch'}, use_global_device_ids=true, to_apply=%region_10.11 | all-reduce | flops 8192 | bytes 65536 | tf_op jit(solution)/shard_map/psum | solution.py:46
  156.3 8.7 %fusion.8 = f32[512]{0:T(512)S(1)} fusion(f32[512,8192]{1,0:T(8,128)} %get-tuple-element.10, f32[8192]{0:T(1024)S(1)} %psum.73, f32[512]{0:T(512)S(1)} %psum.72, f32[8192]{0:T(1024)S(1)} %psum.71), kind=kLoop, calls=%fused_computation.15 | loop fusion | flops 16776704 | bytes 16846848 | tf_op jit(solution)/shard_map/reduce_sum | solution.py:48
  165.1 13.6 %psum.74 = f32[512]{0:T(512)S(1)} all-reduce(f32[512]{0:T(512)S(1)} %fusion.8), channel_id=1, replica_groups=mesh['batch'=4,'proto'=8] {'proto'}, use_global_device_ids=true, to_apply=%region_12.13 | all-reduce | flops 512 | bytes 4096 | tf_op jit(solution)/shard_map/psum | solution.py:48
  178.6 7.8 %fusion.9 = f32[8192]{0:T(1024)S(1)} fusion(f32[512,8192]{1,0:T(8,128)} %get-tuple-element.10, f32[512]{0:T(512)S(1)} %psum.74, f32[8192]{0:T(1024)S(1)} %psum.73, f32[512]{0:T(512)S(1)} %psum.72, f32[8192]{0:T(1024)S(1)} %psum.71), kind=kLoop, calls=%fused_computation.16 | loop fusion | flops 20963328 | bytes 16879616 | tf_op jit(solution)/shard_map/reduce_sum | solution.py:46
  186.4 14.1 %psum.75 = f32[8192]{0:T(1024)S(1)} all-reduce(f32[8192]{0:T(1024)S(1)} %fusion.9), channel_id=1, replica_groups=mesh['batch'=4,'proto'=8] {'batch'}, use_global_device_ids=true, to_apply=%region_14.15 | all-reduce | flops 8192 | bytes 65536 | tf_op jit(solution)/shard_map/psum | solution.py:46
  200.5 8.4 %fusion.10 = f32[512]{0:T(512)S(1)} fusion(f32[512,8192]{1,0:T(8,128)} %get-tuple-element.10, f32[8192]{0:T(1024)S(1)} %psum.75, f32[512]{0:T(512)S(1)} %psum.74, f32[8192]{0:T(1024)S(1)} %psum.73, f32[512]{0:T(512)S(1)} %psum.72, f32[8192]{0:T(1024)S(1)} %psum.71), kind=kLoop, calls=%fused_computation.17 | loop fusion | flops 25165312 | bytes 16881664 | tf_op jit(solution)/shard_map/reduce_sum | solution.py:48
  209.0 7.2 %exponential_reduce_fusion = (f32[512]{0:T(512)S(1)}, f32[512,8192]{1,0:T(8,128)}) fusion(bf16[256,512]{1,0:T(8,128)(2,1)S(1)} %fusion.17, bf16[256,8192]{1,0:T(8,128)(2,1)S(1)} %copy-done.1), kind=kOutput, calls=%fused_computation.12 | convolution fusion | flops 2155871744 | bytes 21235712 | tf_op jit(solution)/shard_map/dot_general | solution.py:19
  216.1 13.8 %all-reduce = (f32[512]{0:T(512)S(1)}, f32[512]{0:T(512)S(1)}) all-reduce(f32[512]{0:T(512)S(1)} %get-tuple-element.7, f32[512]{0:T(512)S(1)} %fusion.10), channel_id=1, replica_groups=mesh['batch'=4,'proto'=8] {'proto'}, use_global_device_ids=true, to_apply=%region_3.4 | all-reduce | flops 1024 | bytes 8192 | tf_op jit(solution)/shard_map/psum | solution.py:53
  229.9 15.3 %multiply_reduce_fusion = (f32[]{:T(128)}, bf16[512,8192]{1,0:T(8,128)(2,1)S(1)}) fusion(f32[512,8192]{1,0:T(8,128)} %get-tuple-element.8, f32[512]{0:T(512)S(1)} %log.3, f32[512,8192]{1,0:T(8,128)} %get-tuple-element.10, f32[512]{0:T(512)S(1)} %get-tuple-element.4, f32[8192]{0:T(1024)S(1)} %psum.75, f32[512]{0:T(512)S(1)} %psum.74, f32[8192]{0:T(1024)S(1)} %psum.73, ...), kind=kLoop, calls=%fused_computation.9 | loop fusion | flops 54525952 | bytes 42049540 | tf_op jit(solution)/shard_map/reduce_sum | solution.py:55
  251.6 9.0 %fusion.26 = f32[256,8192]{1,0:T(8,128)} fusion(bf16[256,512]{1,0:T(8,128)(2,1)S(1)} %fusion.17, bf16[512,8192]{1,0:T(8,128)(2,1)} %copy-done.3), kind=kOutput, calls=%fused_computation.53 | convolution fusion | flops 2147483648 | bytes 17039360 | tf_op jit(solution)/shard_map/dot_general | solution.py:68
  261.3 38.0 %psum.79 = f32[]{:T(128)} all-reduce(f32[]{:T(128)S(6)} %neg.3), channel_id=1, replica_groups=mesh['batch'=4,'proto'=8] {'batch','proto'}, use_global_device_ids=true, to_apply=%region_24.25 | all-reduce | flops 1 | bytes 8 | tf_op jit(solution)/shard_map/psum | solution.py:56
  300.8 15.5 %psum.78 = f32[512]{0:T(512)S(1)} all-reduce(f32[512]{0:T(512)S(1)} %fusion.22), channel_id=1, replica_groups=mesh['batch'=4,'proto'=8] {'proto'}, use_global_device_ids=true, to_apply=%region_22.23 | all-reduce | flops 512 | bytes 4096 | tf_op jit(solution)/shard_map/psum | solution.py:83
  317.8 51.2 %reduce-scatter.3.cloned.1.call-done = f32[64,8192]{1,0:T(8,128)} async-done(((f32[256,8192]{1,0:T(8,128)}), f32[64,8192]{1,0:T(8,128)}) %reduce-scatter.3.cloned.1.call-update) | async-done | bytes 2097168 | tf_op jit(solution)/shard_map/reduce_scatter | solution.py:67
  371.1 15.4 %psum.77 = f32[8192]{0:T(1024)S(1)} all-reduce(f32[8192]{0:T(1024)S(1)} %fusion.13), channel_id=1, replica_groups=mesh['batch'=4,'proto'=8] {'batch'}, use_global_device_ids=true, to_apply=%region_19.20 | all-reduce | flops 8192 | bytes 65536 | tf_op jit(solution)/shard_map/psum | solution.py:82
  (40 shorter events, 24.1 us)
Async XLA Ops:
  7.2 78.8 %copy-start.4 = (bf16[64,8192]{1,0:T(8,128)(2,1)S(1)}, bf16[64,8192]{1,0:T(8,128)(2,1)}, u32[]{:S(2)}) copy-start(bf16[64,8192]{1,0:T(8,128)(2,1)} %param.5) | copy-start | bytes 3145732
  7.2 292.7 %reduce-scatter.5.cloned.1.call-start = ((), (), s32[]{:S(2)}) async-start(), calls=%async_computation.3 | async-start | bytes 589824 | tf_op jit(solution)/shard_map/reduce_scatter | solution.py:74
  7.2 27.3 %collective-permute-start = (bf16[64,8192]{1,0:T(8,128)(2,1)}, bf16[64,8192]{1,0:T(8,128)(2,1)S(1)}, u32[]{:S(2)}, u32[]{:S(2)}) collective-permute-start(bf16[64,8192]{1,0:T(8,128)(2,1)} %param.5), channel_id=1, source_target_pairs={{0,8},{8,16},{16,24},{24,0},{1,9},{9,17},{17,25},{25,1},{2,10},{10... | collective-permute-start | bytes 3145736 | tf_op jit(solution)/shard_map/ppermute | solution.py:31
  34.6 25.2 %collective-permute-start.1 = (bf16[64,8192]{1,0:T(8,128)(2,1)S(1)}, bf16[64,8192]{1,0:T(8,128)(2,1)S(1)}, u32[]{:S(2)}, u32[]{:S(2)}) collective-permute-start(bf16[64,8192]{1,0:T(8,128)(2,1)S(1)} %collective-permute-done), channel_id=1, source_target_pairs={{0,8},{8,16},{16,24},{24,0},{1,9},{9,17},{17,25},{25,1},{2,10},{10... | collective-permute-start | bytes 3145736 | tf_op jit(solution)/shard_map/ppermute | solution.py:31
  59.8 24.4 %collective-permute-start.2 = (bf16[64,8192]{1,0:T(8,128)(2,1)S(1)}, bf16[64,8192]{1,0:T(8,128)(2,1)S(1)}, u32[]{:S(2)}, u32[]{:S(2)}) collective-permute-start(bf16[64,8192]{1,0:T(8,128)(2,1)S(1)} %collective-permute-done.1), channel_id=1, source_target_pairs={{0,8},{8,16},{16,24},{24,0},{1,9},{9,17},{17,25},{25,1},{2,10},{10... | collective-permute-start | bytes 3145736 | tf_op jit(solution)/shard_map/ppermute | solution.py:31
  87.8 2.0 copy-start
  200.5 8.4 %copy-start.1 = (bf16[256,8192]{1,0:T(8,128)(2,1)S(1)}, bf16[256,8192]{1,0:T(8,128)(2,1)}, u32[]{:S(2)}) copy-start(bf16[256,8192]{1,0:T(8,128)(2,1)} %copy-done) | copy-start | bytes 12582916
  229.9 18.5 %copy-start.2 = (bf16[256,8192]{1,0:T(8,128)(2,1)S(1)}, bf16[256,8192]{1,0:T(8,128)(2,1)}, u32[]{:S(2)}) copy-start(bf16[256,8192]{1,0:T(8,128)(2,1)} %copy-done) | copy-start | bytes 12582916
  245.2 3.2 copy-start.3
  251.6 117.4 %reduce-scatter.3.cloned.1.call-start = ((), (), s32[]{:S(2)}) async-start(), calls=%async_computation.2 | async-start | bytes 10485760 | tf_op jit(solution)/shard_map/reduce_scatter | solution.py:67
Sparse Core Ops, SparseCore 0:
  251.7 28.9 reduce-scatter.4
  283.8 85.2 reduce-scatter.2
